TPU v7x, 32 devices: a whole 2x2x4 slice. The times are simulated.
32 devices in a mesh: rep: 4 (over z), px: 4 (over x, core), py: 2 (over y).
Axes of the slice: x: 2, y: 2, z: 4, core: 2. Of those that a mesh axis runs over, the one named last changes fastest.
Arguments:
- state: float32 [12, 2, 192, 96, 256], P('rep', None, 'px', 'py'), parts along dimension 0, may hold values from -6 to 6
- cotangent: float32 [12, 2, 192, 96, 256], P('rep', None, 'px', 'py'), parts along dimension 0, may hold values from -6 to 6
- w_in: bfloat16 [512, 192], replicated, may hold values from -0.4375 to 0.4375
- b_in: float32 [512], replicated, may hold values from -5 to 5
- w_out: bfloat16 [192, 512], replicated, may hold values from -0.25 to 0.25
Outputs:
- state_grad: float32 [12, 2, 192, 96, 256], P('rep', None, 'px', 'py'), parts along dimension 0
- grad_in: float32 [512, 768], P(('px', 'py'), 'rep'), parts along dimension 1
- grad_out: float32 [768, 512], P('rep', ('px', 'py')), parts along dimension 0
- grad_bias: float32 [4, 512], P('rep', ('px', 'py')), parts along dimension 0
There are 4 independent parts, one for each index of `rep`. A program takes and returns all parts, laid end to end along the dimension named above; an argument that names none is the same for every part. Nothing has to cross between parts.
All inputs are finite; a program needn't handle non-finite values.
Results may differ from a plain program's by a relative error of at most 0.0065.
The roundings to bfloat16 on the way count: a program that leaves them out, or rounds other values in their place, can miss the bound.
Values may be sent and summed in bfloat16 or wider, within the bound.
A program may use at most 448 MiB of HBM per device.

v0:
```python
import math
import jax
import jax.numpy as jnp
from jax import lax
from jax.sharding import PartitionSpec as P

PATCH = 4
NU_DT = 5e-05
TIME_STEP = 0.01
FORCING = 20.0


def angles(leading, trailing, length):
    product = leading[:, None] * trailing[None, :] % length
    phases = product.astype(jnp.float32) * (2.0 * math.pi / length)
    factor = 1.0 / math.sqrt(length)
    return (jnp.cos(phases) * factor, jnp.sin(phases) * factor)


def mode_ids(count, length):
    counter = jnp.arange(count, dtype=jnp.int32)
    return jnp.where(counter < count // 2, counter, counter + length - count)


def mode_table(modes, length, direction):
    cosine, sine_part = angles(modes, jnp.arange(length, dtype=jnp.int32), length)
    top_rows = jnp.stack([cosine, direction * sine_part], axis=1)
    low_rows = jnp.stack([-direction * sine_part, cosine], axis=1)
    return jnp.stack([top_rows, low_rows], axis=0).astype(jnp.bfloat16)


def complex_table(length, direction):
    return mode_table(jnp.arange(length, dtype=jnp.int32), length, direction)


def real_table(length, mode_count):
    cosine, sine_part = angles(
        jnp.arange(mode_count, dtype=jnp.int32), jnp.arange(length, dtype=jnp.int32), length
    )
    return jnp.stack([cosine, -sine_part], axis=0).astype(jnp.bfloat16)


def box_order(length, span):
    counter = jnp.arange(length, dtype=jnp.int32)
    local = counter % span
    rows = span // PATCH
    return counter - local + local % rows * PATCH + local // rows


def signed(counter, length):
    return jnp.where(counter < length // 2, counter, counter - length).astype(jnp.float32)


def factors(ky_ids, kz_ids, length, ky_count):
    cutoff = length // 3
    wave_y = signed(ky_ids, ky_count)[:, None, None]
    wave_z = kz_ids.astype(jnp.float32)[None, :, None]
    wave_x = signed(jnp.arange(length, dtype=jnp.int32), length)[None, None, :]
    retained = (
        (jnp.abs(wave_x) <= cutoff) & (jnp.abs(wave_y) <= cutoff) & (wave_z <= cutoff)
    ).astype(jnp.float32)
    square = wave_x * wave_x + wave_y * wave_y + wave_z * wave_z
    damping = jnp.exp(-NU_DT * square)
    weight = jnp.where(kz_ids[None, :, None] == 0, 1.0, 2.0).astype(jnp.float32)
    return ((wave_x, wave_y, wave_z), retained, damping, weight, square)


def cross(former, latter):
    return [
        former[1] * latter[2] - former[2] * latter[1],
        former[2] * latter[0] - former[0] * latter[2],
        former[0] * latter[1] - former[1] * latter[0],
    ]


def curl_modes(waves, spectra):
    real_part = cross(waves, [spectra[slot, 0] for slot in range(3)])
    imag_part = cross(waves, [spectra[slot, 1] for slot in range(3)])
    return jnp.stack([jnp.stack([-imag_part[slot], real_part[slot]]) for slot in range(3)])


def project(waves, square, spectra):
    dotted = waves[0] * spectra[0] + waves[1] * spectra[1] + waves[2] * spectra[2]
    along_k = dotted / jnp.maximum(square, 1.0)
    return jnp.stack([spectra[slot] - waves[slot] * along_k for slot in range(3)])


def to_physical(spectra):
    channels, paired, width_y, width_z, length = spectra.shape
    parts_x = lax.axis_size("px")
    parts_y = lax.axis_size("py")
    order_y = box_order(length, length)
    order_z = box_order(length, length)
    inverse = complex_table(length, 1.0)
    y_table = mode_table(mode_ids(width_y * parts_x, length), length, 1.0)[..., order_y].reshape(
        2, parts_x, width_y, 2, length
    )
    z_table = real_table(length, width_z * parts_y)[..., order_z].reshape(
        2, parts_y, width_z, length
    )
    flat = spectra.astype(jnp.bfloat16).reshape(channels, paired, width_y * width_z, length)
    along_x = jnp.einsum(
        "crpn,rnsx->csxp", flat, inverse, preferred_element_type=jnp.float32
    ).astype(jnp.bfloat16)
    along_x = along_x.reshape(channels, 2, length, 1, width_y * width_z)
    moved = lax.all_to_all(along_x, ("px", "py"), split_axis=2, concat_axis=3, tiled=True)
    blocks = moved.reshape(moved.shape[0], 2, moved.shape[2], parts_x, parts_y, width_y, width_z)
    along_y = jnp.einsum(
        "csxjlam,sjaty->cxtlmy", blocks, y_table, preferred_element_type=jnp.float32
    ).astype(jnp.bfloat16)
    return jnp.einsum(
        "cxtlmy,tlmz->cxyz", along_y, z_table, preferred_element_type=jnp.float32
    ).astype(jnp.bfloat16)


def to_spectral(field, ky_count, mode_count):
    channels, span_x, span_y, length = field.shape
    parts_x = lax.axis_size("px")
    parts_y = lax.axis_size("py")
    width_y = ky_count // parts_x
    width_z = mode_count // parts_y
    order_y = box_order(length, span_y)
    order_z = box_order(length, length)
    forward = complex_table(length, -1.0)
    y_table = (
        mode_table(mode_ids(ky_count, length), length, -1.0)
        .transpose(0, 3, 2, 1)[:, order_y]
        .reshape(2, length, 2, parts_x, width_y)
    )
    z_table = real_table(length, mode_count)[..., order_z].reshape(2, parts_y, width_z, length)
    along_z = jnp.einsum(
        "cxyz,rlmz->crlmxy", field, z_table, preferred_element_type=jnp.float32
    ).astype(jnp.bfloat16)
    along_y = jnp.einsum(
        "crlmxy,rysja->csxjlam", along_z, y_table, preferred_element_type=jnp.float32
    ).astype(jnp.bfloat16)
    along_y = along_y.reshape(channels, 2, span_x, parts_x * parts_y, width_y * width_z)
    moved = lax.all_to_all(along_y, ("px", "py"), split_axis=3, concat_axis=2, tiled=True)
    number = moved.shape[0]
    flat = moved.reshape(number, 2, length, -1)
    along_x = jnp.einsum("csxp,sxtn->ctpn", flat, forward, preferred_element_type=jnp.float32)
    return along_x.reshape(number, 2, width_y, width_z, length)


def to_boxes(field):
    channels, span_x, span_y, span_z = field.shape
    tiles = field.reshape(
        channels, span_x // PATCH, PATCH, PATCH, span_y // PATCH, PATCH, span_z // PATCH
    )
    return tiles.transpose(0, 2, 3, 5, 1, 4, 6).reshape(channels * PATCH**3, -1)


def from_boxes(box_values, layout):
    channels, span_x, span_y, span_z = layout
    tiles = box_values.reshape(
        channels, PATCH, PATCH, PATCH, span_x // PATCH, span_y // PATCH, span_z // PATCH
    )
    return tiles.transpose(0, 4, 1, 2, 5, 3, 6).reshape(layout)


def closure_terms(velocity, force_adj, w_in, b_in, w_out):
    features = to_boxes(velocity)
    adjoints = to_boxes(force_adj)
    pre_act = jnp.dot(w_in, features, preferred_element_type=jnp.float32) + b_in[:, None]
    hidden = jax.nn.silu(pre_act).astype(jnp.bfloat16)
    sigmoid = jax.nn.sigmoid(pre_act)
    hidden_adj = FORCING * jnp.dot(w_out.T, adjoints, preferred_element_type=jnp.float32)
    pre_adj = (hidden_adj * sigmoid * (1.0 + pre_act * (1.0 - sigmoid))).astype(jnp.bfloat16)
    grad_in = jnp.dot(pre_adj, features.T, preferred_element_type=jnp.float32)
    grad_out = FORCING * jnp.dot(adjoints, hidden.T, preferred_element_type=jnp.float32)
    grad_bias = jnp.sum(pre_adj.astype(jnp.float32), axis=1)[None, :]
    feat_adj = jnp.dot(w_in.T, pre_adj, preferred_element_type=jnp.float32).astype(jnp.bfloat16)
    feat_adj = lax.optimization_barrier(from_boxes(feat_adj, velocity.shape))
    return (feat_adj, grad_in, grad_out, grad_bias)


def field_cross(former, latter):
    return cross(
        [former[slot].astype(jnp.float32) for slot in range(3)],
        [latter[slot].astype(jnp.float32) for slot in range(3)],
    )


def shards(state, cotangent, w_in, b_in, w_out):
    width_y = state.shape[2]
    width_z = state.shape[3]
    length = state.shape[4]
    ky_count = width_y * lax.axis_size("px")
    ky_ids = lax.axis_index("px") * width_y + jnp.arange(width_y, dtype=jnp.int32)
    kz_ids = lax.axis_index("py") * width_z + jnp.arange(width_z, dtype=jnp.int32)
    waves, retained, damping, weight, square = factors(ky_ids, kz_ids, length, ky_count)
    kept = retained * state
    force_spec = TIME_STEP * retained * project(waves, square, damping * cotangent)
    modes = width_z * lax.axis_size("py")
    force_adj = to_physical(force_spec)
    velocity = to_physical(weight * kept)
    vorticity = to_physical(weight * curl_modes(waves, kept))
    vort_adj = jnp.stack(field_cross(force_adj, velocity)).astype(jnp.bfloat16)
    spec_vort = to_spectral(vort_adj, ky_count, modes)
    feat_adj, grad_in, grad_out, grad_bias = closure_terms(velocity, force_adj, w_in, b_in, w_out)
    turned = field_cross(vorticity, force_adj)
    vel_adj = jnp.stack([feat_adj[slot].astype(jnp.float32) + turned[slot] for slot in range(3)])
    spec_vel = to_spectral(vel_adj.astype(jnp.bfloat16), ky_count, modes)
    state_grad = damping * cotangent + weight * retained * (spec_vel + curl_modes(waves, spec_vort))
    grad_in, grad_out, grad_bias = (
        lax.psum_scatter(grad_in, ("px", "py"), scatter_dimension=0, tiled=True),
        lax.psum_scatter(grad_out, ("px", "py"), scatter_dimension=1, tiled=True),
        lax.psum_scatter(grad_bias, ("px", "py"), scatter_dimension=1, tiled=True),
    )
    return (state_grad, grad_in, grad_out, grad_bias)


def solution(mesh):
    return jax.shard_map(
        shards,
        mesh=mesh,
        in_specs=(
            P("rep", None, "px", "py", None),
            P("rep", None, "px", "py", None),
            P(),
            P(),
            P(),
        ),
        out_specs=(
            P("rep", None, "px", "py", None),
            P(("px", "py"), "rep"),
            P("rep", ("px", "py")),
            P("rep", ("px", "py")),
        ),
        check_vma=False,
    )
```

profile of v0, /device:TPU:0, one launch (start us, length us, event | category | flops | bytes accessed | tf_op | source)
XLA Modules:
  0.0 1128.6 jit_solution(6317094853116231177)
XLA Ops:
  13.9 6.8 broadcast_multiply_fusion.1
  20.8 2.4 multiply_subtract_fusion.2
  23.2 2.9 copy-done.1
  26.0 9.3 multiply_subtract_fusion.1
  39.0 7.2 fusion.75
  46.3 23.6 %copy.174 = bf16[3,2,256,1,2304]{4,1,3,0,2:T(2,128)(2,1)} copy(bf16[3,2,256,1,2304]{4,2,0,1,3:T(8,128)(2,1)S(1)} %fusion.75) | data formatting | bytes 14155776 | tf_op jit(solution)/shard_map/reshape | solution.py:105
  69.9 16.6 %all-to-all-start = ((bf16[3,2,256,1,2304]{4,1,3,0,2:T(2,128)(2,1)}), bf16[3,2,256,1,2304]{4,1,3,0,2:T(2,128)(2,1)}, u32[]{:S(2)}, u32[]{:S(2)}) async-start(bf16[3,2,256,1,2304]{4,1,3,0,2:T(2,128)(2,1)} %copy.174), calls=%async_computation | async-start | bytes 14155776 | tf_op jit(solution)/shard_map/all_to_all | solution.py:106
  86.9 12.8 %multiply_convert_fusion = (bf16[3,2,48,48,256]{4,3,2,1,0:T(8,128)(2,1)S(1)}, f32[3,2,48,48,256]{4,3,2,1,0:T(8,128)}) fusion(f32[48]{0:T(128)S(1)} %copy-done.28, f32[3,2,48,48,256]{4,3,2,1,0:T(8,128)} %param.5, f32[48,48,256]{2,1,0:T(8,128)S(1)} %and_convert_fusion), kind=kLoop, calls=%fused_computation.59 | loop fusion | flops 10616832 | bytes 37748928 | tf_op jit(solution)/shard_map/convert_element_type | solution.py:101
  99.7 5.9 fusion.74
  105.6 27.6 %copy.180 = bf16[3,2,256,1,2304]{4,1,3,0,2:T(2,128)(2,1)} copy(bf16[3,2,256,1,2304]{4,2,0,1,3:T(8,128)(2,1)} %fusion.74) | data formatting | bytes 14155776 | tf_op jit(solution)/shard_map/reshape | solution.py:105
  133.2 33.0 %all-to-all-done = bf16[3,2,256,1,2304]{4,1,3,0,2:T(2,128)(2,1)} async-done(((bf16[3,2,256,1,2304]{4,1,3,0,2:T(2,128)(2,1)}), bf16[3,2,256,1,2304]{4,1,3,0,2:T(2,128)(2,1)}, u32[]{:S(2)}, u32[]{:S(2)}) %all-to-all-start) | async-done | bytes 7077920 | tf_op jit(solution)/shard_map/all_to_all | solution.py:106
  166.2 4.8 all-to-all-start.1
  181.0 9.7 fusion.155
  190.7 7.1 fusion.88
  197.8 6.6 fusion.78
  204.4 24.0 %copy.187 = bf16[3,2,256,1,2304]{4,1,3,0,2:T(2,128)(2,1)} copy(bf16[3,2,256,1,2304]{4,2,0,1,3:T(8,128)(2,1)S(1)} %fusion.78) | data formatting | bytes 14155776 | tf_op jit(solution)/shard_map/reshape | solution.py:105
  230.2 9.8 copy.331
  240.1 28.9 %reshape.1131 = bf16[3,2,32,4,2,48,48]{6,5,4,3,2,1,0:T(8,128)(2,1)} reshape(bf16[3,2,32,8,1,2304]{5,3,2,1,0,4:T(8,128)(2,1)} %bitcast.414) | data formatting | bytes 14155776 | tf_op jit(solution)/shard_map/reshape | solution.py:107
  269.0 4.8 all-to-all-start.2
  273.9 9.8 copy.330
  283.7 29.0 %reshape.1136 = bf16[3,2,32,4,2,48,48]{6,5,4,3,2,1,0:T(8,128)(2,1)} reshape(bf16[3,2,32,8,1,2304]{5,3,2,1,0,4:T(8,128)(2,1)} %bitcast.415) | data formatting | bytes 14155776 | tf_op jit(solution)/shard_map/reshape | solution.py:107
  312.7 16.2 %bitcast_convert_fusion.3 = bf16[3,32,256,256]{3,2,1,0:T(8,128)(2,1)} fusion(bf16[2,4,48,2,256,1,1,1]{4,2,1,3,0,7,6,5:T(8,128)(2,1)S(1)} %bitcast.429, bf16[2,2,48,256,1,1]{3,2,1,0,5,4:T(8,128)(2,1)S(1)} %bitcast.432, bf16[3,2,32,4,2,48,48]{6,5,4,3,2,1,0:T(8,128)(2,1)} %reshape.1136), kind=kOutput, calls=%fused_computation.21 | convolution fusion | flops 6050807808 | bytes 20152320 | tf_op jit(solution)/shard_map/cxtlmy,tlmz->cxyz/dot_general | solution.py:111
  328.9 36.2 %reshape.1137 = bf16[3,8,4,4,64,4,64]{6,5,4,3,2,1,0:T(4,128)(2,1)} reshape(bf16[3,32,256,256]{3,2,1,0:T(8,128)(2,1)} %bitcast_convert_fusion.3) | data formatting | bytes 25165824 | tf_op jit(solution)/shard_map/reshape | solution.py:147
  365.0 16.4 %bitcast_convert_fusion.4 = bf16[3,32,256,256]{3,2,1,0:T(8,128)(2,1)} fusion(bf16[2,4,48,2,256,1,1,1]{4,2,1,3,0,7,6,5:T(8,128)(2,1)S(1)} %bitcast.430, bf16[2,2,48,256,1,1]{3,2,1,0,5,4:T(8,128)(2,1)S(1)} %bitcast.433, bf16[3,2,32,4,2,48,48]{6,5,4,3,2,1,0:T(8,128)(2,1)} %reshape.1131), kind=kOutput, calls=%fused_computation.22 | convolution fusion | flops 6050807808 | bytes 20152320 | tf_op jit(solution)/shard_map/cxtlmy,tlmz->cxyz/dot_general | solution.py:111
  381.4 36.2 %reshape.1132 = bf16[3,8,4,4,64,4,64]{6,5,4,3,2,1,0:T(4,128)(2,1)} reshape(bf16[3,32,256,256]{3,2,1,0:T(8,128)(2,1)} %bitcast_convert_fusion.4) | data formatting | bytes 25165824 | tf_op jit(solution)/shard_map/reshape | solution.py:147
  417.6 11.3 %fusion.49 = (bf16[1,32,256,256]{3,2,1,0:T(8,128)(2,1)S(1)}, bf16[1,32,256,256]{3,2,1,0:T(8,128)(2,1)S(1)}, bf16[1,32,256,256]{3,2,1,0:T(8,128)(2,1)S(1)}) fusion(bf16[3,32,256,256]{3,2,1,0:T(8,128)(2,1)} %bitcast_convert_fusion.3, bf16[3,32,256,256]{3,2,1,0:T(8,128)(2,1)} %bitcast_convert_fusion.4), kind=kLoop, calls=%fused_computation.86 | loop fusion | flops 37748736 | bytes 37748736 | tf_op jit(solution)/shard_map/convert
  428.9 6.5 fusion.27
  435.4 15.6 %fusion.11 = bf16[3,2,32,4,2,48,48]{6,5,2,4,0,3,1:T(8,128)(2,1)} fusion(bf16[2,2,48,3,32,256]{5,2,0,4,1,3:T(8,128)(2,1)} %fusion.27, bf16[2,256,2,4,48,1,1,1]{1,4,3,2,0,7,6,5:T(8,128)(2,1)} %bitcast.427), kind=kOutput, calls=%fused_computation.27 | convolution fusion | flops 3627417600 | bytes 16908288 | tf_op jit(solution)/shard_map/crlmxy,rysja->csxjlam/dot_general | solution.py:134
  451.0 18.1 %copy.270 = bf16[3,2,32,4,2,48,48]{6,5,2,1,0,4,3:T(8,128)(2,1)} copy(bf16[3,2,32,4,2,48,48]{6,5,2,4,0,3,1:T(8,128)(2,1)} %fusion.11) | data formatting | bytes 14155776 | tf_op jit(solution)/shard_map/reshape | solution.py:137
  469.1 26.4 %reshape.1212 = bf16[3,2,32,8,2304]{4,2,1,0,3:T(8,128)(2,1)} reshape(bf16[3,2,32,4,2,48,48]{6,5,2,1,0,4,3:T(8,128)(2,1)} %copy.270) | data formatting | bytes 14155776 | tf_op jit(solution)/shard_map/reshape | solution.py:137
  495.5 22.6 %copy.327 = bf16[3,8,4,4,64,4,64]{6,4,1,5,3,2,0:T(8,128)(2,1)} copy(bf16[3,8,4,4,64,4,64]{6,5,4,3,2,1,0:T(4,128)(2,1)} %reshape.1137) | data formatting | bytes 25165824 | tf_op jit(solution)/shard_map/reshape | solution.py:147
  518.2 29.1 %reshape.1138 = bf16[192,32768]{1,0:T(8,128)(2,1)} reshape(bf16[3,4,4,4,8,64,64]{6,5,4,3,2,1,0:T(8,128)(2,1)} %bitcast.405) | data formatting | bytes 25165824 | tf_op jit(solution)/shard_map/reshape | solution.py:150
  547.3 4.8 all-to-all-start.4
  552.1 9.8 copy.329
  562.0 29.2 %reshape.1142 = bf16[3,2,32,4,2,48,48]{6,5,4,3,2,1,0:T(8,128)(2,1)} reshape(bf16[3,2,32,8,1,2304]{5,3,2,1,0,4:T(8,128)(2,1)} %bitcast.416) | data formatting | bytes 14155776 | tf_op jit(solution)/shard_map/reshape | solution.py:107
  591.1 16.2 %bitcast_convert_fusion.2 = bf16[3,32,256,256]{3,2,1,0:T(8,128)(2,1)} fusion(bf16[2,4,48,2,256,1,1,1]{4,2,1,3,0,7,6,5:T(8,128)(2,1)S(1)} %bitcast.431, bf16[2,2,48,256,1,1]{3,2,1,0,5,4:T(8,128)(2,1)S(1)} %bitcast.435, bf16[3,2,32,4,2,48,48]{6,5,4,3,2,1,0:T(8,128)(2,1)} %reshape.1142), kind=kOutput, calls=%fused_computation.20 | convolution fusion | flops 6050807808 | bytes 20152320 | tf_op jit(solution)/shard_map/cxtlmy,tlmz->cxyz/dot_general | solution.py:111
  607.3 22.6 %copy.328 = bf16[3,8,4,4,64,4,64]{6,4,1,5,3,2,0:T(8,128)(2,1)} copy(bf16[3,8,4,4,64,4,64]{6,5,4,3,2,1,0:T(4,128)(2,1)} %reshape.1132) | data formatting | bytes 25165824 | tf_op jit(solution)/shard_map/reshape | solution.py:147
  629.9 29.1 %reshape.1133 = bf16[192,32768]{1,0:T(8,128)(2,1)} reshape(bf16[3,4,4,4,8,64,64]{6,5,4,3,2,1,0:T(8,128)(2,1)} %bitcast.406) | data formatting | bytes 25165824 | tf_op jit(solution)/shard_map/reshape | solution.py:150
  659.0 27.8 %fusion.156 = f32[32768,512]{1,0:T(8,128)} fusion(bf16[192,32768]{1,0:T(8,128)(2,1)} %reshape.1138, bf16[512,192]{0,1:T(8,128)(2,1)S(1)} %copy-done), kind=kOutput, calls=%fused_computation.263 | convolution fusion | flops 6442450944 | bytes 79888384 | tf_op jit(solution)/shard_map/dot_general | solution.py:164
  686.8 46.9 %convert_reduce_fusion = (f32[512]{0:T(512)S(1)}, bf16[512,32768]{0,1:T(8,128)(2,1)}) fusion(f32[32768,512]{1,0:T(8,128)} %fusion.156, f32[512]{0:T(512)S(1)} %copy-done.32, bf16[192,32768]{1,0:T(8,128)(2,1)} %reshape.1133, bf16[192,512]{1,0:T(8,128)(2,1)S(1)} %copy-done.31), kind=kOutput, calls=%fused_computation.14 | convolution fusion | flops 6660554240 | bytes 113446912 | tf_op jit(solution)/shard_map/dot_general | solution.py:167
  734.7 21.2 %fusion.7 = bf16[192,32768]{1,0:T(8,128)(2,1)} fusion(bf16[512,32768]{0,1:T(8,128)(2,1)} %get-tuple-element.59, bf16[512,192]{0,1:T(8,128)(2,1)S(1)} %copy-done), kind=kOutput, calls=%fused_computation.16 | convolution fusion | flops 6448742400 | bytes 46333952 | tf_op jit(solution)/shard_map/dot_general | solution.py:172
  755.8 30.9 %reshape.1139 = bf16[3,4,4,4,8,64,64]{6,5,4,3,2,1,0:T(8,128)(2,1)} reshape(bf16[192,32768]{1,0:T(8,128)(2,1)} %fusion.7) | data formatting | bytes 25165824 | tf_op jit(solution)/shard_map/reshape | solution.py:155
  786.7 29.0 %copy.326 = bf16[3,4,4,4,8,64,64]{6,3,5,2,1,4,0:T(4,128)(2,1)} copy(bf16[3,4,4,4,8,64,64]{6,5,4,3,2,1,0:T(8,128)(2,1)} %reshape.1139) | data formatting | bytes 25165824 | tf_op jit(solution)/shard_map/reshape | solution.py:155
  815.7 35.7 %reshape.1140 = bf16[3,32,256,256]{3,2,1,0:T(8,128)(2,1)} reshape(bf16[3,8,4,4,64,4,64]{6,5,4,3,2,1,0:T(4,128)(2,1)} %bitcast.407) | data formatting | bytes 25165824 | tf_op jit(solution)/shard_map/reshape | solution.py:158
  851.4 18.5 %fusion.44 = (bf16[1,32,256,256]{3,2,1,0:T(8,128)(2,1)}, bf16[1,32,256,256]{3,2,1,0:T(8,128)(2,1)}, bf16[1,32,256,256]{3,2,1,0:T(8,128)(2,1)}) fusion(bf16[3,32,256,256]{3,2,1,0:T(8,128)(2,1)} %reshape.1140, bf16[3,32,256,256]{3,2,1,0:T(8,128)(2,1)} %bitcast_convert_fusion.2, bf16[3,32,256,256]{3,2,1,0:T(8,128)(2,1)} %bitcast_convert_fusion.4), kind=kLoop, calls=%fused_computation.81 | loop fusion | flops 50331648 | bytes 50331648 | tf_op jit(solution)/shard_map/convert.3
  870.0 9.6 fusion.22
  879.6 39.9 %fusion.10 = bf16[3,2,32,4,2,48,48]{6,5,2,4,0,3,1:T(8,128)(2,1)} fusion(bf16[2,2,48,3,32,256]{5,2,0,4,1,3:T(8,128)(2,1)} %fusion.22, bf16[2,256,2,4,48,1,1,1]{1,4,3,2,0,7,6,5:T(8,128)(2,1)S(1)} %bitcast.428), kind=kOutput, calls=%fused_computation.26 | convolution fusion | flops 3627417600 | bytes 16908288 | tf_op jit(solution)/shard_map/crlmxy,rysja->csxjlam/dot_general | solution.py:134
  919.5 15.4 %fusion.157 = f32[512,192]{1,0:T(8,128)} fusion(bf16[512,32768]{0,1:T(8,128)(2,1)} %get-tuple-element.59, bf16[192,32768]{1,0:T(8,128)(2,1)S(1)} %bitcast.413), kind=kOutput, calls=%fused_computation.264 | convolution fusion | flops 6442450944 | bytes 46530560 | tf_op jit(solution)/shard_map/dot_general | solution.py:169
  934.9 18.2 %copy.263 = bf16[3,2,32,4,2,48,48]{6,5,2,1,0,4,3:T(8,128)(2,1)} copy(bf16[3,2,32,4,2,48,48]{6,5,2,4,0,3,1:T(8,128)(2,1)} %fusion.10) | data formatting | bytes 14155776 | tf_op jit(solution)/shard_map/reshape | solution.py:137
  953.0 26.2 %reshape.1211 = bf16[3,2,32,8,2304]{4,2,1,0,3:T(8,128)(2,1)} reshape(bf16[3,2,32,4,2,48,48]{6,5,2,1,0,4,3:T(8,128)(2,1)} %copy.263) | data formatting | bytes 14155776 | tf_op jit(solution)/shard_map/reshape | solution.py:137
  979.3 4.9 all-to-all-start.3
  984.2 31.2 %fusion.92 = f32[192,512]{0,1:T(8,128)} fusion(bf16[192,32768]{1,0:T(8,128)(2,1)} %reshape.1133, f32[32768,512]{1,0:T(8,128)} %fusion.156, f32[512]{0:T(512)S(1)} %copy-done.32), kind=kOutput, calls=%fused_computation.154 | convolution fusion | flops 6543212544 | bytes 80087040 | tf_op jit(solution)/shard_map/dot_general | solution.py:170
  1016.8 3.7 copy.203
  1020.5 7.4 convolution_bitcast_fusion
  1027.9 15.3 %copy.205 = f32[3,2,2304,256]{3,2,1,0:T(8,128)} copy(f32[3,2,2304,256]{2,3,0,1:T(8,128)} %convolution_bitcast_fusion) | data formatting | bytes 28311552 | tf_op jit(solution)/shard_map/csxp,sxtn->ctpn/transpose | solution.py:141
  1043.2 10.4 subtract_negate_fusion.1
  1053.7 13.9 %all-to-all-done.3 = bf16[3,2,32,8,2304]{4,2,1,0,3:T(8,128)(2,1)} async-done(((bf16[3,2,32,8,2304]{4,2,1,0,3:T(8,128)(2,1)}), bf16[3,2,32,8,2304]{4,2,1,0,3:T(8,128)(2,1)}, u32[]{:S(2)}, u32[]{:S(2)}) %all-to-all-start.3) | async-done | bytes 7077920 | tf_op jit(solution)/shard_map/all_to_all | solution.py:138
  1067.5 3.6 copy.196
  1071.2 7.4 convolution_bitcast_fusion.1
  1078.5 15.5 %copy.198 = f32[3,2,2304,256]{3,2,1,0:T(8,128)} copy(f32[3,2,2304,256]{2,3,0,1:T(8,128)} %convolution_bitcast_fusion.1) | data formatting | bytes 28311552 | tf_op jit(solution)/shard_map/csxp,sxtn->ctpn/transpose | solution.py:141
  1094.1 2.9 maximum_bitcast_fusion.5
  1097.8 2.7 maximum_bitcast_fusion.6
  1100.6 2.7 maximum_bitcast_fusion.4
  1106.8 14.8 %fusion.21 = f32[3,2,48,48,256]{4,3,2,1,0:T(8,128)} fusion(f32[3,2,48,48,256]{4,3,2,1,0:T(8,128)S(1)} %bitcast.411, f32[1,2,48,48,256]{4,3,2,1,0:T(8,128)} %maximum_bitcast_fusion.6, f32[1,2,48,48,256]{4,3,2,1,0:T(8,128)S(1)} %maximum_bitcast_fusion.5, f32[1,2,48,48,256]{4,3,2,1,0:T(8,128)} %maximum_bitcast_fusion.4, f32[48,48,256]{2,1,0:T(8,128)} %and_select_fusion, ...), kind=kLoop, calls=%fused_computation.55 | loop fusion | flops 21233664 | bytes 61341696 | tf_op jit(solution)/shard_map/add | solution.py:204
  (137 shorter events, 29.3 us)
Async XLA Ops:
  7.2 651.8 %copy-start = (bf16[512,192]{0,1:T(8,128)(2,1)S(1)}, bf16[512,192]{0,1:T(8,128)(2,1)}, u32[]{:S(2)}) copy-start(bf16[512,192]{0,1:T(8,128)(2,1)} %param.7) | copy-start | bytes 589828
  8.3 12.4 %copy-start.29 = (pred[48]{0:T(512)(128)(4,1)}, pred[48]{0:T(512)(128)(4,1)S(1)}, u32[]{:S(2)}) copy-start(pred[48]{0:T(512)(128)(4,1)S(1)} %broadcast_compare_fusion) | copy-start | bytes 148
  8.9 162.3 %copy-start.20 = (f32[48]{0:T(128)}, f32[48]{0:T(128)S(1)}, u32[]{:S(2)}) copy-start(f32[48]{0:T(128)S(1)} %get-tuple-element.68) | copy-start | bytes 580
  13.8 6.9 copy-start.2
  13.9 6.9 copy-start.22
  13.9 6.9 copy-start.25
  20.7 5.3 copy-start.1
  36.1 1.1 copy-start.16
  39.0 7.2 copy-start.12
  39.0 7.2 copy-start.14
  69.9 16.6 %copy-start.17 = (pred[48,256]{1,0:T(8,128)(4,1)S(1)}, pred[48,256]{1,0:T(8,128)(4,1)}, u32[]{:S(2)}) copy-start(pred[48,256]{1,0:T(8,128)(4,1)} %copy-done.16) | copy-start | bytes 36868
  69.9 16.6 %copy-start.30 = (pred[48]{0:T(512)(128)(4,1)S(1)}, pred[48]{0:T(512)(128)(4,1)}, u32[]{:S(2)}) copy-start(pred[48]{0:T(512)(128)(4,1)} %copy-done.29) | copy-start | bytes 148
  69.9 17.0 %copy-start.28 = (f32[48]{0:T(128)S(1)}, f32[48]{0:T(128)}, u32[]{:S(2)}) copy-start(f32[48]{0:T(128)} %get-tuple-element.60) | copy-start | bytes 580
  69.9 96.3 %all-to-all-start = ((bf16[3,2,256,1,2304]{4,1,3,0,2:T(2,128)(2,1)}), bf16[3,2,256,1,2304]{4,1,3,0,2:T(2,128)(2,1)}, u32[]{:S(2)}, u32[]{:S(2)}) async-start(bf16[3,2,256,1,2304]{4,1,3,0,2:T(2,128)(2,1)} %copy.174), calls=%async_computation | async-start | bytes 14155776 | tf_op jit(solution)/shard_map/all_to_all | solution.py:106
  86.9 12.8 %copy-start.13 = (bf16[1,256,2,256]{1,3,0,2:T(8,128)(2,1)S(1)}, bf16[1,256,2,256]{1,3,0,2:T(8,128)(2,1)}, u32[]{:S(2)}) copy-start(bf16[1,256,2,256]{1,3,0,2:T(8,128)(2,1)} %copy-done.12) | copy-start | bytes 786436
  86.9 12.8 %copy-start.15 = (bf16[1,256,2,256]{1,3,0,2:T(8,128)(2,1)S(1)}, bf16[1,256,2,256]{1,3,0,2:T(8,128)(2,1)}, u32[]{:S(2)}) copy-start(bf16[1,256,2,256]{1,3,0,2:T(8,128)(2,1)} %copy-done.14) | copy-start | bytes 786436
  133.2 38.1 %copy-start.23 = (f32[48]{0:T(128)S(1)}, f32[48]{0:T(128)}, u32[]{:S(2)}) copy-start(f32[48]{0:T(128)} %get-tuple-element.69) | copy-start | bytes 580
  166.2 102.8 %all-to-all-start.1 = ((bf16[3,2,256,1,2304]{4,1,3,0,2:T(2,128)(2,1)}), bf16[3,2,256,1,2304]{4,1,3,0,2:T(2,128)(2,1)}, u32[]{:S(2)}, u32[]{:S(2)}) async-start(bf16[3,2,256,1,2304]{4,1,3,0,2:T(2,128)(2,1)} %copy.180), calls=%async_computation.1 | async-start | bytes 14155776 | tf_op jit(solution)/shard_map/all_to_all | solution.py:106
  181.0 184.1 %copy-start.10 = (bf16[2,192,2,256]{3,1,2,0:T(8,128)(2,1)}, bf16[2,192,2,256]{3,1,2,0:T(8,128)(2,1)S(1)}, u32[]{:S(2)}) copy-start(bf16[2,192,2,256]{3,1,2,0:T(8,128)(2,1)S(1)} %copy.172) | copy-start | bytes 1179652
  181.0 9.7 copy-start.26
  269.0 278.2 %all-to-all-start.2 = ((bf16[3,2,256,1,2304]{4,1,3,0,2:T(2,128)(2,1)}), bf16[3,2,256,1,2304]{4,1,3,0,2:T(2,128)(2,1)}, u32[]{:S(2)}, u32[]{:S(2)}) async-start(bf16[3,2,256,1,2304]{4,1,3,0,2:T(2,128)(2,1)} %copy.187), calls=%async_computation.2 | async-start | bytes 14155776 | tf_op jit(solution)/shard_map/all_to_all | solution.py:106
  283.7 29.0 %copy-start.18 = (bf16[2,96,256]{2,1,0:T(8,128)(2,1)S(1)}, bf16[2,96,256]{2,1,0:T(8,128)(2,1)}, u32[]{:S(2)}) copy-start(bf16[2,96,256]{2,1,0:T(8,128)(2,1)} %copy.170) | copy-start | bytes 294916
  547.3 432.0 %all-to-all-start.4 = ((bf16[3,2,32,8,2304]{4,2,1,0,3:T(8,128)(2,1)}), bf16[3,2,32,8,2304]{4,2,1,0,3:T(8,128)(2,1)}, u32[]{:S(2)}, u32[]{:S(2)}) async-start(bf16[3,2,32,8,2304]{4,2,1,0,3:T(8,128)(2,1)} %reshape.1212), calls=%async_computation.4 | async-start | bytes 14155776 | tf_op jit(solution)/shard_map/all_to_all | solution.py:138
  552.1 463.4 %reduce-scatter.10.cloned.1.call-start = ((), (), s32[]{:S(2)}) async-start(), calls=%async_computation.10 | async-start | bytes 294912
  562.0 29.2 %copy-start.11 = (bf16[2,192,2,256]{3,1,2,0:T(8,128)(2,1)S(1)}, bf16[2,192,2,256]{3,1,2,0:T(8,128)(2,1)}, u32[]{:S(2)}) copy-start(bf16[2,192,2,256]{3,1,2,0:T(8,128)(2,1)} %copy-done.10) | copy-start | bytes 1179652
  659.0 27.8 %copy-start.31 = (bf16[192,512]{1,0:T(8,128)(2,1)S(1)}, bf16[192,512]{1,0:T(8,128)(2,1)}, u32[]{:S(2)}) copy-start(bf16[192,512]{1,0:T(8,128)(2,1)} %param.9) | copy-start | bytes 589828
  659.0 27.8 %copy-start.32 = (f32[512]{0:T(512)S(1)}, f32[512]{0:T(512)}, u32[]{:S(2)}) copy-start(f32[512]{0:T(512)} %param.8) | copy-start | bytes 6148
  734.6 387.0 %reduce-scatter.6.cloned.1.call-start = ((), (), s32[]{:S(2)}) async-start(), calls=%async_computation.8 | async-start | bytes 589824 | tf_op jit(solution)/shard_map/reduce_scatter | solution.py:206
  851.4 18.6 %copy-start.19 = (bf16[2,96,256]{2,1,0:T(8,128)(2,1)S(1)}, bf16[2,96,256]{2,1,0:T(8,128)(2,1)}, u32[]{:S(2)}) copy-start(bf16[2,96,256]{2,1,0:T(8,128)(2,1)} %copy.170) | copy-start | bytes 294916
  870.0 9.6 copy-start.9
  870.0 49.5 %slice-start.4 = ((s8[12582912]{0:T(1024)(128)(4,1)}), s8[4194304]{0:T(1024)(128)(4,1)S(1)}, s32[]{:S(2)}) async-start(s8[12582912]{0:T(1024)(128)(4,1)} %bitcast.412), calls=%async_computation.15 | async-start | bytes 8388608
  870.0 49.5 %slice-start.5 = ((s8[12582912]{0:T(1024)(128)(4,1)}), s8[4194304]{0:T(1024)(128)(4,1)S(1)}, s32[]{:S(2)}) async-start(s8[12582912]{0:T(1024)(128)(4,1)} %bitcast.412), calls=%async_computation.16 | async-start | bytes 8388608
  879.6 39.9 %slice-start.6 = ((s8[12582912]{0:T(1024)(128)(4,1)}), s8[4194304]{0:T(1024)(128)(4,1)S(1)}, s32[]{:S(2)}) async-start(s8[12582912]{0:T(1024)(128)(4,1)} %bitcast.412), calls=%async_computation.17 | async-start | bytes 8388608
  979.3 88.2 %all-to-all-start.3 = ((bf16[3,2,32,8,2304]{4,2,1,0,3:T(8,128)(2,1)}), bf16[3,2,32,8,2304]{4,2,1,0,3:T(8,128)(2,1)}, u32[]{:S(2)}, u32[]{:S(2)}) async-start(bf16[3,2,32,8,2304]{4,2,1,0,3:T(8,128)(2,1)} %reshape.1211), calls=%async_computation.3 | async-start | bytes 14155776 | tf_op jit(solution)/shard_map/all_to_all | solution.py:138
  984.2 137.4 %reduce-scatter.8.cloned.1.call-start = ((), (), s32[]{:S(2)}) async-start(), calls=%async_computation.9 | async-start | bytes 589824 | tf_op jit(solution)/shard_map/reduce_scatter | solution.py:207
  1016.8 3.7 copy-start.7
  1016.8 3.7 copy-start.8
  1027.9 15.3 %copy-start.21 = (f32[48]{0:T(128)S(1)}, f32[48]{0:T(128)}, u32[]{:S(2)}) copy-start(f32[48]{0:T(128)} %copy-done.20) | copy-start | bytes 580
  1027.9 15.3 %copy-start.24 = (f32[48]{0:T(128)S(1)}, f32[48]{0:T(128)}, u32[]{:S(2)}) copy-start(f32[48]{0:T(128)} %get-tuple-element.69) | copy-start | bytes 580
  1027.9 15.3 %copy-start.27 = (f32[256]{0:T(256)S(1)}, f32[256]{0:T(256)}, u32[]{:S(2)}) copy-start(f32[256]{0:T(256)} %fusion.140) | copy-start | bytes 3076
  1094.0 3.1 copy-start.5
  1094.0 3.8 copy-start.6
  1094.0 9.3 slice-start
  1094.0 10.3 slice-start.1
  1096.9 3.6 copy-start.4
  1097.8 7.8 slice-start.2
  1100.6 5.8 copy-start.3
  1100.6 6.2 slice-start.3
Sparse Core Ops, SparseCore 0:
  734.7 35.8 reduce-scatter.9
  979.4 41.3 reduce-scatter.5
  1024.5 36.3 reduce-scatter.7
where the time goes:
time: 1150 us; the launch traced here: 1130 us
  local copies, waits for them, and re-layouts  618 us (54%)
  matrix products  297 us (26%)
  other arithmetic  115 us (10%)
  waiting for transfers between devices  46.9 us (4%)
  starting transfers between devices  36 us (3%)
  between operations  14.9 us (1%)
    reshape x4, local copies, waits for them, and re-layouts, to_boxes(): field.reshape(channels, span_x // PATCH, PATCH, PATCH, span_y // PATCH, P...  118 us
    reshape x4, local copies, waits for them, and re-layouts, to_spectral(): along_y.reshape(channels, 2, span_x, parts_x * parts_y, width_y * width_z)  88.9 us
    reshape x3, local copies, waits for them, and re-layouts, to_physical(): moved.reshape(moved.shape[0], 2, moved.shape[2], parts_x, parts_y, width_...  87.1 us
    reshape x3, local copies, waits for them, and re-layouts, to_physical(): along_x = along_x.reshape(channels, 2, length, 1, width_y * width_z)  75.2 us
    reshape x2, local copies, waits for them, and re-layouts, from_boxes(): box_values.reshape(channels, PATCH, PATCH, PATCH, span_x // PATCH, span_y...  59.9 us
    reshape x2, local copies, waits for them, and re-layouts, to_boxes(): tiles.transpose(0, 2, 3, 5, 1, 4, 6).reshape(channels * PATCH ** 3, -1)  58.2 us
    dot_general x2, matrix products, to_spectral(): jnp.einsum('crlmxy,rysja->csxjlam', along_z, y_table, preferred_element_t...  55.5 us
    dot_general x3, matrix products, to_physical(): jnp.einsum('cxtlmy,tlmz->cxyz', along_y, z_table, preferred_element_type=...  48.8 us
  transfers between devices with their start and end apart: 8, of which 2 were waited for; matrix products, arithmetic and copies ran while one was open for 85% of the time, Pallas kernels for 0%

commit v1 on v0

--- a/solution.py
+++ b/solution.py
@@ -1,3 +1,4 @@
+import functools
 import math
 import jax
 import jax.numpy as jnp
@@ -8,6 +9,17 @@
 NU_DT = 5e-05
 TIME_STEP = 0.01
 FORCING = 20.0
+
+
+def edges_begin(u_in, along_axis):
+    v_now = lax.axis_size(along_axis)
+    x_next = jnp.split(u_in, v_now, axis=2)
+    item_now = jnp.stack(x_next)
+    arr_out = lax.all_to_all(item_now, axis_name=along_axis, split_axis=0, concat_axis=0)
+    return jnp.concatenate(arr_out, axis=3)
+
+
+_clear_edges = functools.partial(edges_begin, along_axis=("px", "py"))
 
 
 def angles(leading, trailing, length):
@@ -103,7 +115,7 @@
         "crpn,rnsx->csxp", flat, inverse, preferred_element_type=jnp.float32
     ).astype(jnp.bfloat16)
     along_x = along_x.reshape(channels, 2, length, 1, width_y * width_z)
-    moved = lax.all_to_all(along_x, ("px", "py"), split_axis=2, concat_axis=3, tiled=True)
+    moved = _clear_edges(along_x)
     blocks = moved.reshape(moved.shape[0], 2, moved.shape[2], parts_x, parts_y, width_y, width_z)
     along_y = jnp.einsum(
         "csxjlam,sjaty->cxtlmy", blocks, y_table, preferred_element_type=jnp.float32

time: 1150 us -> 1080 us (0.939)
  local copies, waits for them, and re-layouts: 618 us -> 560 us
    reshape x6 -> x0, local copies, waits for them, and re-layouts: 162 us -> none  [the longest x3 87.1 us: to_physical(): moved.reshape(moved.shape[0], 2, moved.shape[2], parts_x, parts_y, width_...]
    another operation x0 -> x6, local copies, waits for them, and re-layouts: none -> 91.2 us  [the longest x3 87.1 us: to_physical(): moved.reshape(moved.shape[0], 2, moved.shape[2], parts_x, parts_y, width_...]
    unnamed x82 -> x125, local copies, waits for them, and re-layouts: 9.59 us -> 40.4 us
    all_to_all x3 -> x0, local copies, waits for them, and re-layouts: 29.5 us -> none  [to_physical(): lax.all_to_all(along_x, ('px', 'py'), split_axis=2, concat_axis=3, tiled=...]
  transfers between devices with their start and end apart: 8 -> 8, of which waited for: 2 -> 3; matrix products, arithmetic and copies ran while one was open for 85% -> 86% of each run, Pallas kernels for 0% -> 0%
where the time goes in v1:
time: 1080 us; the launch traced here: 1060 us
  local copies, waits for them, and re-layouts  560 us (52%)
  matrix products  299 us (28%)
  other arithmetic  114 us (11%)
  waiting for transfers between devices  50.7 us (5%)
  starting transfers between devices  25.1 us (2%)
  between operations  14.7 us (1%)
    reshape x4, local copies, waits for them, and re-layouts, to_boxes(): field.reshape(channels, span_x // PATCH, PATCH, PATCH, span_y // PATCH, P...  118 us
    reshape x4, local copies, waits for them, and re-layouts, to_spectral(): along_y.reshape(channels, 2, span_x, parts_x * parts_y, width_y * width_z)  88.7 us
    another operation x3, local copies, waits for them, and re-layouts, to_physical(): moved.reshape(moved.shape[0], 2, moved.shape[2], parts_x, parts_y, width_...  87.1 us
    reshape x2, local copies, waits for them, and re-layouts, from_boxes(): box_values.reshape(channels, PATCH, PATCH, PATCH, span_x // PATCH, span_y...  59.9 us
    reshape x2, local copies, waits for them, and re-layouts, to_boxes(): tiles.transpose(0, 2, 3, 5, 1, 4, 6).reshape(channels * PATCH ** 3, -1)  58.2 us
    dot_general x2, matrix products, to_spectral(): jnp.einsum('crlmxy,rysja->csxjlam', along_z, y_table, preferred_element_t...  55.7 us
    dot_general x3, matrix products, to_physical(): jnp.einsum('cxtlmy,tlmz->cxyz', along_y, z_table, preferred_element_type=...  48.7 us
    dot_general x1, matrix products, closure_terms(): jnp.dot(w_out.T, adjoints, preferred_element_type=jnp.float32)  46.6 us
  transfers between devices with their start and end apart: 8, of which 3 were waited for; matrix products, arithmetic and copies ran while one was open for 86% of the time, Pallas kernels for 0%

profile of v1, /device:TPU:0, one launch (start us, length us, event | category | flops | bytes accessed | tf_op | source)
XLA Modules:
  0.0 1063.3 jit_solution(6464011748373633378)
XLA Ops:
  13.9 6.8 broadcast_multiply_fusion.1
  23.1 2.9 copy-done.1
  26.0 9.4 multiply_subtract_fusion.1
  39.1 7.2 fusion.75
  54.4 5.6 all-to-all-start
  62.0 13.7 %multiply_convert_fusion = (bf16[3,2,48,48,256]{4,3,2,1,0:T(8,128)(2,1)}, f32[3,2,48,48,256]{4,3,2,1,0:T(8,128)}) fusion(f32[48]{0:T(128)S(1)} %copy-done.37, f32[3,2,48,48,256]{4,3,2,1,0:T(8,128)} %param.5, f32[48,48,256]{2,1,0:T(8,128)S(1)} %and_convert_fusion), kind=kLoop, calls=%fused_computation.59 | loop fusion | flops 10616832 | bytes 37748928 | tf_op jit(solution)/shard_map/convert_element_type | solution.py:113
  75.7 7.1 fusion.74
  83.2 2.6 copy-done.12
  85.7 2.9 copy-done.11
  88.6 9.5 fusion.179
  99.6 2.9 fusion.106
  109.0 3.7 fusion.88
  112.8 7.1 fusion.78
  119.8 19.6 %all-to-all-done = bf16[8,3,2,32,1,2304]{5,3,1,2,4,0:T(8,128)(2,1)} async-done(((bf16[8,3,2,32,1,2304]{5,3,1,2,4,0:T(8,128)(2,1)}), bf16[8,3,2,32,1,2304]{5,3,1,2,4,0:T(8,128)(2,1)}, u32[]{:S(2)}, u32[]{:S(2)}) %all-to-all-start) | async-done | bytes 7077920 | tf_op jit(solution)/shard_map/all_to_all | solution.py:18
  139.4 4.8 all-to-all-start.1
  152.1 3.6 gather_fusion
  158.8 3.6 gather_fusion.2
  165.6 2.5 fusion.102
  177.5 29.0 %reshape_reshape.9 = bf16[3,2,32,4,2,48,48]{6,5,2,0,1,4,3:T(8,128)(2,1)} reshape(bf16[3,2,32,8,1,2304]{5,2,0,1,4,3:T(8,128)(2,1)} %bitcast.41) | data formatting | bytes 14155776 | tf_op jit(solution)/shard_map/reshape;reshape | solution.py:119
  206.4 16.9 %all-to-all-done.1 = bf16[8,3,2,32,1,2304]{5,3,1,2,4,0:T(8,128)(2,1)} async-done(((bf16[8,3,2,32,1,2304]{5,3,1,2,4,0:T(8,128)(2,1)}), bf16[8,3,2,32,1,2304]{5,3,1,2,4,0:T(8,128)(2,1)}, u32[]{:S(2)}, u32[]{:S(2)}) %all-to-all-start.1) | async-done | bytes 7077920 | tf_op jit(solution)/shard_map/all_to_all | solution.py:18
  223.3 5.0 all-to-all-start.2
  228.4 29.0 %reshape_reshape.10 = bf16[3,2,32,4,2,48,48]{6,5,2,0,1,4,3:T(8,128)(2,1)} reshape(bf16[3,2,32,8,1,2304]{5,2,0,1,4,3:T(8,128)(2,1)} %bitcast.68) | data formatting | bytes 14155776 | tf_op jit(solution)/shard_map/reshape;reshape | solution.py:119
  257.4 16.2 %bitcast_convert_fusion.3 = bf16[3,32,256,256]{3,2,1,0:T(8,128)(2,1)} fusion(bf16[2,4,48,2,256,1,1,1]{4,2,1,3,0,7,6,5:T(8,128)(2,1)S(1)} %bitcast.515, bf16[2,2,48,256,1,1]{3,2,1,0,5,4:T(8,128)(2,1)S(1)} %bitcast.518, bf16[3,2,32,4,2,48,48]{6,5,2,0,1,4,3:T(8,128)(2,1)} %reshape_reshape.10), kind=kOutput, calls=%fused_computation.21 | convolution fusion | flops 6050807808 | bytes 20152320 | tf_op jit(solution)/shard_map/cxtlmy,tlmz->cxyz/dot_general | solution.py:123
  273.6 36.2 %reshape.1134 = bf16[3,8,4,4,64,4,64]{6,5,4,3,2,1,0:T(4,128)(2,1)} reshape(bf16[3,32,256,256]{3,2,1,0:T(8,128)(2,1)} %bitcast_convert_fusion.3) | data formatting | bytes 25165824 | tf_op jit(solution)/shard_map/reshape | solution.py:159
  309.7 16.3 %bitcast_convert_fusion.4 = bf16[3,32,256,256]{3,2,1,0:T(8,128)(2,1)} fusion(bf16[2,4,48,2,256,1,1,1]{4,2,1,3,0,7,6,5:T(8,128)(2,1)S(1)} %bitcast.516, bf16[2,2,48,256,1,1]{3,2,1,0,5,4:T(8,128)(2,1)S(1)} %bitcast.519, bf16[3,2,32,4,2,48,48]{6,5,2,0,1,4,3:T(8,128)(2,1)} %reshape_reshape.9), kind=kOutput, calls=%fused_computation.22 | convolution fusion | flops 6050807808 | bytes 20152320 | tf_op jit(solution)/shard_map/cxtlmy,tlmz->cxyz/dot_general | solution.py:123
  326.0 36.1 %reshape.1129 = bf16[3,8,4,4,64,4,64]{6,5,4,3,2,1,0:T(4,128)(2,1)} reshape(bf16[3,32,256,256]{3,2,1,0:T(8,128)(2,1)} %bitcast_convert_fusion.4) | data formatting | bytes 25165824 | tf_op jit(solution)/shard_map/reshape | solution.py:159
  362.2 11.7 %fusion.49 = (bf16[1,32,256,256]{3,2,1,0:T(8,128)(2,1)S(1)}, bf16[1,32,256,256]{3,2,1,0:T(8,128)(2,1)S(1)}, bf16[1,32,256,256]{3,2,1,0:T(8,128)(2,1)S(1)}) fusion(bf16[3,32,256,256]{3,2,1,0:T(8,128)(2,1)} %bitcast_convert_fusion.3, bf16[3,32,256,256]{3,2,1,0:T(8,128)(2,1)} %bitcast_convert_fusion.4), kind=kLoop, calls=%fused_computation.86 | loop fusion | flops 37748736 | bytes 37748736 | tf_op jit(solution)/shard_map/convert
  373.9 6.5 fusion.27
  380.4 15.6 %fusion.11 = bf16[3,2,32,4,2,48,48]{6,5,2,4,0,3,1:T(8,128)(2,1)} fusion(bf16[2,2,48,3,32,256]{5,2,0,4,1,3:T(8,128)(2,1)} %fusion.27, bf16[2,256,2,4,48,1,1,1]{1,4,3,2,0,7,6,5:T(8,128)(2,1)} %bitcast.513), kind=kOutput, calls=%fused_computation.27 | convolution fusion | flops 3627417600 | bytes 16908288 | tf_op jit(solution)/shard_map/crlmxy,rysja->csxjlam/dot_general | solution.py:146
  396.0 18.1 %copy.194 = bf16[3,2,32,4,2,48,48]{6,5,2,1,0,4,3:T(8,128)(2,1)} copy(bf16[3,2,32,4,2,48,48]{6,5,2,4,0,3,1:T(8,128)(2,1)} %fusion.11) | data formatting | bytes 14155776 | tf_op jit(solution)/shard_map/reshape | solution.py:149
  414.1 26.2 %reshape.1209 = bf16[3,2,32,8,2304]{4,2,1,0,3:T(8,128)(2,1)} reshape(bf16[3,2,32,4,2,48,48]{6,5,2,1,0,4,3:T(8,128)(2,1)} %copy.194) | data formatting | bytes 14155776 | tf_op jit(solution)/shard_map/reshape | solution.py:149
  440.3 22.6 %copy.248 = bf16[3,8,4,4,64,4,64]{6,4,1,5,3,2,0:T(8,128)(2,1)} copy(bf16[3,8,4,4,64,4,64]{6,5,4,3,2,1,0:T(4,128)(2,1)} %reshape.1134) | data formatting | bytes 25165824 | tf_op jit(solution)/shard_map/reshape | solution.py:159
  463.0 29.1 %reshape.1135 = bf16[192,32768]{1,0:T(8,128)(2,1)} reshape(bf16[3,4,4,4,8,64,64]{6,5,4,3,2,1,0:T(8,128)(2,1)} %bitcast.492) | data formatting | bytes 25165824 | tf_op jit(solution)/shard_map/reshape | solution.py:162
  492.1 4.8 all-to-all-start.4
  496.9 29.1 %reshape_reshape.11 = bf16[3,2,32,4,2,48,48]{6,5,2,0,1,4,3:T(8,128)(2,1)} reshape(bf16[3,2,32,8,1,2304]{5,2,0,1,4,3:T(8,128)(2,1)} %bitcast.101) | data formatting | bytes 14155776 | tf_op jit(solution)/shard_map/reshape;reshape | solution.py:119
  526.0 16.2 %bitcast_convert_fusion.2 = bf16[3,32,256,256]{3,2,1,0:T(8,128)(2,1)} fusion(bf16[2,4,48,2,256,1,1,1]{4,2,1,3,0,7,6,5:T(8,128)(2,1)S(1)} %bitcast.517, bf16[2,2,48,256,1,1]{3,2,1,0,5,4:T(8,128)(2,1)S(1)} %bitcast.521, bf16[3,2,32,4,2,48,48]{6,5,2,0,1,4,3:T(8,128)(2,1)} %reshape_reshape.11), kind=kOutput, calls=%fused_computation.20 | convolution fusion | flops 6050807808 | bytes 20152320 | tf_op jit(solution)/shard_map/cxtlmy,tlmz->cxyz/dot_general | solution.py:123
  542.2 22.6 %copy.249 = bf16[3,8,4,4,64,4,64]{6,4,1,5,3,2,0:T(8,128)(2,1)} copy(bf16[3,8,4,4,64,4,64]{6,5,4,3,2,1,0:T(4,128)(2,1)} %reshape.1129) | data formatting | bytes 25165824 | tf_op jit(solution)/shard_map/reshape | solution.py:159
  564.8 29.1 %reshape.1130 = bf16[192,32768]{1,0:T(8,128)(2,1)} reshape(bf16[3,4,4,4,8,64,64]{6,5,4,3,2,1,0:T(8,128)(2,1)} %bitcast.493) | data formatting | bytes 25165824 | tf_op jit(solution)/shard_map/reshape | solution.py:162
  593.9 27.8 %fusion.180 = f32[32768,512]{1,0:T(8,128)} fusion(bf16[192,32768]{1,0:T(8,128)(2,1)} %reshape.1135, bf16[512,192]{0,1:T(8,128)(2,1)S(1)} %copy-done), kind=kOutput, calls=%fused_computation.308 | convolution fusion | flops 6442450944 | bytes 79888384 | tf_op jit(solution)/shard_map/dot_general | solution.py:176
  621.8 46.6 %convert_reduce_fusion = (f32[512]{0:T(512)S(1)}, bf16[512,32768]{0,1:T(8,128)(2,1)}) fusion(f32[32768,512]{1,0:T(8,128)} %fusion.180, f32[512]{0:T(512)S(1)} %copy-done.41, bf16[192,32768]{1,0:T(8,128)(2,1)} %reshape.1130, bf16[192,512]{1,0:T(8,128)(2,1)S(1)} %copy-done.40), kind=kOutput, calls=%fused_computation.14 | convolution fusion | flops 6660554240 | bytes 113446912 | tf_op jit(solution)/shard_map/dot_general | solution.py:179
  669.3 21.2 %fusion.7 = bf16[192,32768]{1,0:T(8,128)(2,1)} fusion(bf16[512,32768]{0,1:T(8,128)(2,1)} %get-tuple-element.59, bf16[512,192]{0,1:T(8,128)(2,1)S(1)} %copy-done), kind=kOutput, calls=%fused_computation.16 | convolution fusion | flops 6448742400 | bytes 46333952 | tf_op jit(solution)/shard_map/dot_general | solution.py:184
  690.6 30.9 %reshape.1136 = bf16[3,4,4,4,8,64,64]{6,5,4,3,2,1,0:T(8,128)(2,1)} reshape(bf16[192,32768]{1,0:T(8,128)(2,1)} %fusion.7) | data formatting | bytes 25165824 | tf_op jit(solution)/shard_map/reshape | solution.py:167
  721.5 29.0 %copy.247 = bf16[3,4,4,4,8,64,64]{6,3,5,2,1,4,0:T(4,128)(2,1)} copy(bf16[3,4,4,4,8,64,64]{6,5,4,3,2,1,0:T(8,128)(2,1)} %reshape.1136) | data formatting | bytes 25165824 | tf_op jit(solution)/shard_map/reshape | solution.py:167
  750.5 35.7 %reshape.1137 = bf16[3,32,256,256]{3,2,1,0:T(8,128)(2,1)} reshape(bf16[3,8,4,4,64,4,64]{6,5,4,3,2,1,0:T(4,128)(2,1)} %bitcast.494) | data formatting | bytes 25165824 | tf_op jit(solution)/shard_map/reshape | solution.py:170
  786.2 18.6 %fusion.44 = (bf16[1,32,256,256]{3,2,1,0:T(8,128)(2,1)}, bf16[1,32,256,256]{3,2,1,0:T(8,128)(2,1)}, bf16[1,32,256,256]{3,2,1,0:T(8,128)(2,1)}) fusion(bf16[3,32,256,256]{3,2,1,0:T(8,128)(2,1)} %reshape.1137, bf16[3,32,256,256]{3,2,1,0:T(8,128)(2,1)} %bitcast_convert_fusion.2, bf16[3,32,256,256]{3,2,1,0:T(8,128)(2,1)} %bitcast_convert_fusion.4), kind=kLoop, calls=%fused_computation.81 | loop fusion | flops 50331648 | bytes 50331648 | tf_op jit(solution)/shard_map/convert.3
  804.8 9.7 fusion.22
  814.5 40.1 %fusion.10 = bf16[3,2,32,4,2,48,48]{6,5,2,4,0,3,1:T(8,128)(2,1)} fusion(bf16[2,2,48,3,32,256]{5,2,0,4,1,3:T(8,128)(2,1)} %fusion.22, bf16[2,256,2,4,48,1,1,1]{1,4,3,2,0,7,6,5:T(8,128)(2,1)S(1)} %bitcast.514), kind=kOutput, calls=%fused_computation.26 | convolution fusion | flops 3627417600 | bytes 16908288 | tf_op jit(solution)/shard_map/crlmxy,rysja->csxjlam/dot_general | solution.py:146
  854.6 15.4 %fusion.181 = f32[512,192]{1,0:T(8,128)} fusion(bf16[512,32768]{0,1:T(8,128)(2,1)} %get-tuple-element.59, bf16[192,32768]{1,0:T(8,128)(2,1)S(1)} %bitcast.500), kind=kOutput, calls=%fused_computation.309 | convolution fusion | flops 6442450944 | bytes 46530560 | tf_op jit(solution)/shard_map/dot_general | solution.py:181
  869.9 18.2 %copy.187 = bf16[3,2,32,4,2,48,48]{6,5,2,1,0,4,3:T(8,128)(2,1)} copy(bf16[3,2,32,4,2,48,48]{6,5,2,4,0,3,1:T(8,128)(2,1)} %fusion.10) | data formatting | bytes 14155776 | tf_op jit(solution)/shard_map/reshape | solution.py:149
  888.1 26.2 %reshape.1208 = bf16[3,2,32,8,2304]{4,2,1,0,3:T(8,128)(2,1)} reshape(bf16[3,2,32,4,2,48,48]{6,5,2,1,0,4,3:T(8,128)(2,1)} %copy.187) | data formatting | bytes 14155776 | tf_op jit(solution)/shard_map/reshape | solution.py:149
  914.4 4.8 all-to-all-start.3
  919.3 31.1 %fusion.92 = f32[192,512]{0,1:T(8,128)} fusion(bf16[192,32768]{1,0:T(8,128)(2,1)} %reshape.1130, f32[32768,512]{1,0:T(8,128)} %fusion.180, f32[512]{0:T(512)S(1)} %copy-done.41), kind=kOutput, calls=%fused_computation.151 | convolution fusion | flops 6543212544 | bytes 80087040 | tf_op jit(solution)/shard_map/dot_general | solution.py:182
  951.8 3.7 copy.127
  955.5 7.4 convolution_bitcast_fusion
  962.9 15.3 %copy.129 = f32[3,2,2304,256]{3,2,1,0:T(8,128)} copy(f32[3,2,2304,256]{2,3,0,1:T(8,128)} %convolution_bitcast_fusion) | data formatting | bytes 28311552 | tf_op jit(solution)/shard_map/csxp,sxtn->ctpn/transpose | solution.py:153
  978.2 10.3 subtract_negate_fusion.1
  988.5 14.1 %all-to-all-done.3 = bf16[3,2,32,8,2304]{4,2,1,0,3:T(8,128)(2,1)} async-done(((bf16[3,2,32,8,2304]{4,2,1,0,3:T(8,128)(2,1)}), bf16[3,2,32,8,2304]{4,2,1,0,3:T(8,128)(2,1)}, u32[]{:S(2)}, u32[]{:S(2)}) %all-to-all-start.3) | async-done | bytes 7077920 | tf_op jit(solution)/shard_map/all_to_all | solution.py:150
  1002.6 3.6 copy.120
  1006.2 7.4 convolution_bitcast_fusion.1
  1013.6 15.4 %copy.122 = f32[3,2,2304,256]{3,2,1,0:T(8,128)} copy(f32[3,2,2304,256]{2,3,0,1:T(8,128)} %convolution_bitcast_fusion.1) | data formatting | bytes 28311552 | tf_op jit(solution)/shard_map/csxp,sxtn->ctpn/transpose | solution.py:153
  1029.0 2.9 maximum_bitcast_fusion.5
  1032.8 2.7 maximum_bitcast_fusion.6
  1035.5 2.7 maximum_bitcast_fusion.4
  1041.7 14.8 %fusion.21 = f32[3,2,48,48,256]{4,3,2,1,0:T(8,128)} fusion(f32[3,2,48,48,256]{4,3,2,1,0:T(8,128)S(1)} %bitcast.498, f32[1,2,48,48,256]{4,3,2,1,0:T(8,128)} %maximum_bitcast_fusion.6, f32[1,2,48,48,256]{4,3,2,1,0:T(8,128)S(1)} %maximum_bitcast_fusion.5, f32[1,2,48,48,256]{4,3,2,1,0:T(8,128)} %maximum_bitcast_fusion.4, f32[48,48,256]{2,1,0:T(8,128)} %and_select_fusion, ...), kind=kLoop, calls=%fused_computation.55 | loop fusion | flops 21233664 | bytes 61341696 | tf_op jit(solution)/shard_map/add | solution.py:216
  (178 shorter events, 61.3 us)
Async XLA Ops:
  7.2 586.8 %copy-start = (bf16[512,192]{0,1:T(8,128)(2,1)S(1)}, bf16[512,192]{0,1:T(8,128)(2,1)}, u32[]{:S(2)}) copy-start(bf16[512,192]{0,1:T(8,128)(2,1)} %param.7) | copy-start | bytes 589828
  8.3 12.4 %copy-start.38 = (pred[48]{0:T(512)(128)(4,1)}, pred[48]{0:T(512)(128)(4,1)S(1)}, u32[]{:S(2)}) copy-start(pred[48]{0:T(512)(128)(4,1)S(1)} %broadcast_compare_fusion) | copy-start | bytes 148
  8.8 52.0 %copy-start.29 = (f32[48]{0:T(128)}, f32[48]{0:T(128)S(1)}, u32[]{:S(2)}) copy-start(f32[48]{0:T(128)S(1)} %get-tuple-element.68) | copy-start | bytes 580
  13.8 6.9 copy-start.2
  13.8 6.9 copy-start.31
  13.8 6.9 copy-start.34
  20.7 5.3 copy-start.1
  36.1 1.1 copy-start.24
  39.1 7.2 copy-start.18
  39.1 7.2 copy-start.21
  54.4 6.0 copy-start.25
  54.4 6.0 copy-start.39
  54.4 6.4 copy-start.37
  54.4 6.6 copy-start.32
  54.4 85.0 %all-to-all-start = ((bf16[8,3,2,32,1,2304]{5,3,1,2,4,0:T(8,128)(2,1)}), bf16[8,3,2,32,1,2304]{5,3,1,2,4,0:T(8,128)(2,1)}, u32[]{:S(2)}, u32[]{:S(2)}) async-start(bf16[8,3,2,32,1,2304]{5,3,1,2,4,0:T(8,128)(2,1)} %fusion.111), calls=%async_computation | async-start | bytes 14155776 | tf_op jit(solution)/shard_map/all_to_all | solution.py:18
  62.0 13.7 %copy-start.19 = (bf16[1,256,2,256]{1,3,0,2:T(8,128)(2,1)S(1)}, bf16[1,256,2,256]{1,3,0,2:T(8,128)(2,1)}, u32[]{:S(2)}) copy-start(bf16[1,256,2,256]{1,3,0,2:T(8,128)(2,1)} %copy-done.18) | copy-start | bytes 786436
  62.0 13.7 %copy-start.22 = (bf16[1,256,2,256]{1,3,0,2:T(8,128)(2,1)S(1)}, bf16[1,256,2,256]{1,3,0,2:T(8,128)(2,1)}, u32[]{:S(2)}) copy-start(bf16[1,256,2,256]{1,3,0,2:T(8,128)(2,1)} %copy-done.21) | copy-start | bytes 786436
  82.9 2.8 copy-start.12
  85.7 2.9 copy-start.11
  98.0 10.9 %copy-start.4 = (f32[1,1,48,48,256]{4,3,2,1,0:T(8,128)S(1)}, f32[1,1,48,48,256]{4,3,2,1,0:T(8,128)}, u32[]{:S(2)}) copy-start(f32[1,1,48,48,256]{4,3,2,1,0:T(8,128)} %get-tuple-element.27) | copy-start | bytes 7077892
  98.0 10.9 %copy-start.5 = (f32[1,1,48,48,256]{4,3,2,1,0:T(8,128)S(1)}, f32[1,1,48,48,256]{4,3,2,1,0:T(8,128)}, u32[]{:S(2)}) copy-start(f32[1,1,48,48,256]{4,3,2,1,0:T(8,128)} %get-tuple-element.28) | copy-start | bytes 7077892
  98.0 10.9 %copy-start.6 = (f32[1,1,48,48,256]{4,3,2,1,0:T(8,128)S(1)}, f32[1,1,48,48,256]{4,3,2,1,0:T(8,128)}, u32[]{:S(2)}) copy-start(f32[1,1,48,48,256]{4,3,2,1,0:T(8,128)} %get-tuple-element.29) | copy-start | bytes 7077892
  98.0 10.9 %copy-start.7 = (f32[1,1,48,48,256]{4,3,2,1,0:T(8,128)S(1)}, f32[1,1,48,48,256]{4,3,2,1,0:T(8,128)}, u32[]{:S(2)}) copy-start(f32[1,1,48,48,256]{4,3,2,1,0:T(8,128)} %get-tuple-element.30) | copy-start | bytes 7077892
  98.1 10.9 %copy-start.35 = (f32[256]{0:T(256)S(1)}, f32[256]{0:T(256)}, u32[]{:S(2)}) copy-start(f32[256]{0:T(256)} %fusion.164) | copy-start | bytes 3076
  109.0 3.7 copy-start.20
  109.0 3.7 copy-start.23
  139.4 83.9 %all-to-all-start.1 = ((bf16[8,3,2,32,1,2304]{5,3,1,2,4,0:T(8,128)(2,1)}), bf16[8,3,2,32,1,2304]{5,3,1,2,4,0:T(8,128)(2,1)}, u32[]{:S(2)}, u32[]{:S(2)}) async-start(bf16[8,3,2,32,1,2304]{5,3,1,2,4,0:T(8,128)(2,1)} %fusion.103), calls=%async_computation.1 | async-start | bytes 14155776 | tf_op jit(solution)/shard_map/all_to_all | solution.py:18
  144.2 28.2 %slice-start.7 = ((s8[7077888]{0:T(1024)(128)(4,1)}), s8[2883584]{0:T(1024)(128)(4,1)S(1)}, s32[]{:S(2)}) async-start(s8[7077888]{0:T(1024)(128)(4,1)} %bitcast.503), calls=%async_computation.18 | async-start | bytes 5767168
  163.8 146.0 %copy-start.16 = (bf16[2,192,2,256]{3,1,2,0:T(8,128)(2,1)}, bf16[2,192,2,256]{3,1,2,0:T(8,128)(2,1)S(1)}, u32[]{:S(2)}) copy-start(bf16[2,192,2,256]{3,1,2,0:T(8,128)(2,1)S(1)} %copy.102) | copy-start | bytes 1179652
  163.8 8.7 slice-start.8
  223.3 268.7 %all-to-all-start.2 = ((bf16[8,3,2,32,1,2304]{5,3,1,2,4,0:T(8,128)(2,1)}), bf16[8,3,2,32,1,2304]{5,3,1,2,4,0:T(8,128)(2,1)}, u32[]{:S(2)}, u32[]{:S(2)}) async-start(bf16[8,3,2,32,1,2304]{5,3,1,2,4,0:T(8,128)(2,1)} %fusion.95), calls=%async_computation.2 | async-start | bytes 14155776 | tf_op jit(solution)/shard_map/all_to_all | solution.py:18
  228.4 29.0 %copy-start.26 = (bf16[2,96,256]{2,1,0:T(8,128)(2,1)S(1)}, bf16[2,96,256]{2,1,0:T(8,128)(2,1)}, u32[]{:S(2)}) copy-start(bf16[2,96,256]{2,1,0:T(8,128)(2,1)} %copy.100) | copy-start | bytes 294916
  362.2 11.7 %copy-start.27 = (bf16[2,96,256]{2,1,0:T(8,128)(2,1)S(1)}, bf16[2,96,256]{2,1,0:T(8,128)(2,1)}, u32[]{:S(2)}) copy-start(bf16[2,96,256]{2,1,0:T(8,128)(2,1)} %copy.100) | copy-start | bytes 294916
  492.1 422.3 %all-to-all-start.4 = ((bf16[3,2,32,8,2304]{4,2,1,0,3:T(8,128)(2,1)}), bf16[3,2,32,8,2304]{4,2,1,0,3:T(8,128)(2,1)}, u32[]{:S(2)}, u32[]{:S(2)}) async-start(bf16[3,2,32,8,2304]{4,2,1,0,3:T(8,128)(2,1)} %reshape.1209), calls=%async_computation.4 | async-start | bytes 14155776 | tf_op jit(solution)/shard_map/all_to_all | solution.py:150
  496.8 453.6 %reduce-scatter.10.cloned.1.call-start = ((), (), s32[]{:S(2)}) async-start(), calls=%async_computation.10 | async-start | bytes 294912
  496.9 29.1 %copy-start.17 = (bf16[2,192,2,256]{3,1,2,0:T(8,128)(2,1)S(1)}, bf16[2,192,2,256]{3,1,2,0:T(8,128)(2,1)}, u32[]{:S(2)}) copy-start(bf16[2,192,2,256]{3,1,2,0:T(8,128)(2,1)} %copy-done.16) | copy-start | bytes 1179652
  593.9 27.8 %copy-start.40 = (bf16[192,512]{1,0:T(8,128)(2,1)S(1)}, bf16[192,512]{1,0:T(8,128)(2,1)}, u32[]{:S(2)}) copy-start(bf16[192,512]{1,0:T(8,128)(2,1)} %param.9) | copy-start | bytes 589828
  593.9 27.8 %copy-start.41 = (f32[512]{0:T(512)S(1)}, f32[512]{0:T(512)}, u32[]{:S(2)}) copy-start(f32[512]{0:T(512)} %param.8) | copy-start | bytes 6148
  669.3 387.2 %reduce-scatter.6.cloned.1.call-start = ((), (), s32[]{:S(2)}) async-start(), calls=%async_computation.8 | async-start | bytes 589824 | tf_op jit(solution)/shard_map/reduce_scatter | solution.py:218
  786.2 18.6 %copy-start.28 = (bf16[2,96,256]{2,1,0:T(8,128)(2,1)S(1)}, bf16[2,96,256]{2,1,0:T(8,128)(2,1)}, u32[]{:S(2)}) copy-start(bf16[2,96,256]{2,1,0:T(8,128)(2,1)} %copy.100) | copy-start | bytes 294916
  804.8 9.7 copy-start.15
  804.8 49.8 %slice-start.4 = ((s8[12582912]{0:T(1024)(128)(4,1)}), s8[4194304]{0:T(1024)(128)(4,1)S(1)}, s32[]{:S(2)}) async-start(s8[12582912]{0:T(1024)(128)(4,1)} %bitcast.499), calls=%async_computation.15 | async-start | bytes 8388608
  804.8 49.8 %slice-start.5 = ((s8[12582912]{0:T(1024)(128)(4,1)}), s8[4194304]{0:T(1024)(128)(4,1)S(1)}, s32[]{:S(2)}) async-start(s8[12582912]{0:T(1024)(128)(4,1)} %bitcast.499), calls=%async_computation.16 | async-start | bytes 8388608
  814.5 40.1 %slice-start.6 = ((s8[12582912]{0:T(1024)(128)(4,1)}), s8[4194304]{0:T(1024)(128)(4,1)S(1)}, s32[]{:S(2)}) async-start(s8[12582912]{0:T(1024)(128)(4,1)} %bitcast.499), calls=%async_computation.17 | async-start | bytes 8388608
  914.4 88.2 %all-to-all-start.3 = ((bf16[3,2,32,8,2304]{4,2,1,0,3:T(8,128)(2,1)}), bf16[3,2,32,8,2304]{4,2,1,0,3:T(8,128)(2,1)}, u32[]{:S(2)}, u32[]{:S(2)}) async-start(bf16[3,2,32,8,2304]{4,2,1,0,3:T(8,128)(2,1)} %reshape.1208), calls=%async_computation.3 | async-start | bytes 14155776 | tf_op jit(solution)/shard_map/all_to_all | solution.py:150
  919.2 137.3 %reduce-scatter.8.cloned.1.call-start = ((), (), s32[]{:S(2)}) async-start(), calls=%async_computation.9 | async-start | bytes 589824 | tf_op jit(solution)/shard_map/reduce_scatter | solution.py:219
  951.8 3.7 copy-start.13
  951.8 3.7 copy-start.14
  962.9 15.3 %copy-start.30 = (f32[48]{0:T(128)S(1)}, f32[48]{0:T(128)}, u32[]{:S(2)}) copy-start(f32[48]{0:T(128)} %copy-done.29) | copy-start | bytes 580
  962.9 15.3 %copy-start.33 = (f32[48]{0:T(128)S(1)}, f32[48]{0:T(128)}, u32[]{:S(2)}) copy-start(f32[48]{0:T(128)} %get-tuple-element.69) | copy-start | bytes 580
  962.9 15.3 %copy-start.36 = (f32[256]{0:T(256)S(1)}, f32[256]{0:T(256)}, u32[]{:S(2)}) copy-start(f32[256]{0:T(256)} %fusion.164) | copy-start | bytes 3076
  1029.0 3.1 copy-start.9
  1029.0 3.8 copy-start.10
  1029.0 9.3 slice-start
  1029.0 10.3 slice-start.1
  1031.9 3.6 copy-start.8
  1032.8 7.8 slice-start.2
  1035.5 5.8 copy-start.3
  1035.5 6.2 slice-start.3
Sparse Core Ops, SparseCore 0:
  669.4 36.1 reduce-scatter.9
  914.5 41.5 reduce-scatter.5
  959.7 36.3 reduce-scatter.7
